TPU v7x, 32 devices: a whole 2x2x4 slice. The times are simulated.
32 devices in a mesh: tm: 16 (over z, x, core), acct: 2 (over y).
Axes of the slice: x: 2, y: 2, z: 4, core: 2. Of those that a mesh axis runs over, the one named last changes fastest.
Arguments:
- returns: bfloat16 [128, 131072], P('tm'), may hold values from -6 to 6
- start: int32 [1], replicated, may hold values from 0 to 131056
- exposures: bfloat16 [512, 131072], P('acct', 'tm'), may hold values from -0.125 to 0.125
- links: int32 [512], replicated, may hold values from 0 to 127
Outputs:
- cov_block: bfloat16 [16, 131072], P('acct', 'tm')
- house_totals: float32 [16, 128], replicated
All inputs are finite; a program needn't handle non-finite values.
Results may differ from a plain program's by a relative error of at most 0.005.
Values may be sent and summed in bfloat16 or wider, within the bound.
A program may use at most 64 MiB of HBM per device.

v0:
```python
import functools
import math

import jax
import jax.numpy as jnp
from jax import lax
from jax.experimental import pallas as pl
from jax.experimental.pallas import tpu as pltpu
from jax.sharding import PartitionSpec as P

HOUSES = 128
LANES = 128
MESH = pl.DeviceIdType.MESH


def least_divisor(count):
    return min((d for d in range(2, count + 1) if count % d == 0), default=1)


def kernel(
    sizes,
    start_ref, links_ref, tiles_hbm, returns_hbm, exposures_hbm,
    cov_hbm, totals_ref,
    tiles, exps, gathered, blocks, turned, covs, slots1, slots2,
    local_sem, dsend, drecv, bsend, brecv, fsend, frecv, send1, recv1, send2, recv2,
):
    tms, accts, low, rows_dev = sizes
    days, factors = returns_hbm.shape
    all_days = days * tms
    rows = rows_dev * accts
    cols = factors // tms
    piece = cols // accts
    own_accounts = exps.shape[0]
    me, acct = lax.axis_index("tm"), lax.axis_index("acct")
    place, layer = lax.rem(me, low), me // low

    def there(shift):
        return lax.rem(me + shift, tms)

    def at_acct(shift):
        return lax.rem(acct + shift, accts)

    own_cols = pl.ds(pl.multiple_of(me * cols + acct * piece, LANES), piece)
    load_tiles = pltpu.make_async_copy(tiles_hbm, tiles, local_sem.at[2])
    load_tiles.start()
    load_own = pltpu.make_async_copy(returns_hbm.at[:, own_cols], gathered.at[me], local_sem.at[0])
    load_own.start()
    load_exps = pltpu.make_async_copy(exposures_hbm, exps, local_sem.at[1])
    load_exps.start()

    barrier = pltpu.get_barrier_semaphore()
    greeted = 0
    for shift in range(1, tms):
        pl.semaphore_signal(barrier, inc=1, device_id=(there(shift), acct), device_id_type=MESH)
        greeted += 1
    for step in range(low):
        for hop in range(1, accts):
            other = layer * low + lax.rem(place + step, low)
            pl.semaphore_signal(barrier, inc=1, device_id=(other, at_acct(hop)), device_id_type=MESH)
            greeted += 1

    load_tiles.wait()
    tile_count = tiles.shape[0]
    first_tile = lax.div(start_ref[0], LANES)
    window = jnp.concatenate(
        [tiles[first_tile], tiles[jnp.minimum(first_tile + 1, tile_count - 1)]], axis=1
    )
    offset = start_ref[0] - first_tile * LANES
    source = lax.broadcasted_iota(jnp.int32, (2 * LANES, LANES), 0)
    target = lax.broadcasted_iota(jnp.int32, (2 * LANES, LANES), 1)
    pick = jnp.where((source == target + offset) & (target < rows), 1.0, 0.0)
    picked = jnp.dot(window, pick.astype(jnp.bfloat16), preferred_element_type=jnp.float32)

    def raw_weight(day):
        return jnp.exp(-math.log(3.0) * (all_days - 1.0 - day.astype(jnp.float32)) / all_days)

    total = jnp.sum(
        raw_weight(lax.broadcasted_iota(jnp.int32, (days, all_days), 1)), axis=1, keepdims=True
    )
    weights = raw_weight(me * days + lax.broadcasted_iota(jnp.int32, (days, LANES), 0)) / total
    blocks[me] = (picked * weights).astype(jnp.bfloat16)

    pl.semaphore_wait(barrier, greeted)

    shifts = [*range(tms // 2, tms), *range(tms // 2 - 1, 0, -1)]
    sends = []
    for shift in shifts:
        copy = pltpu.make_async_remote_copy(
            src_ref=blocks.at[me], dst_ref=blocks.at[me],
            send_sem=bsend.at[shift], recv_sem=brecv.at[shift],
            device_id=(there(shift), acct), device_id_type=MESH,
        )
        copy.start()
        sends.append(copy)
    last = max(LANES, piece // 2 // LANES * LANES)
    parts = [(at, size) for at, size in ((0, piece - last), (piece - last, last)) if size]

    def direct(index, shift, slot):
        at, size = parts[index]
        to = there(shift)
        return pltpu.make_async_remote_copy(
            src_ref=returns_hbm.at[
                :, pl.ds(pl.multiple_of(to * cols + acct * piece + at, LANES), size)
            ],
            dst_ref=gathered.at[slot, :, pl.ds(at, size)],
            send_sem=dsend.at[index, shift], recv_sem=drecv.at[index, shift],
            device_id=(to, acct), device_id_type=MESH,
        )

    for index in range(len(parts)):
        for shift in shifts:
            copy = direct(index, shift, me)
            copy.start()
            sends.append(copy)

    for shift in shifts:
        block = blocks.at[there(tms - shift)]
        pltpu.make_async_remote_copy(
            src_ref=block, dst_ref=block, send_sem=bsend.at[shift], recv_sem=brecv.at[shift],
            device_id=(there(shift), acct), device_id_type=MESH,
        ).wait_recv()
    turned[...] = blocks[...].astype(jnp.float32).reshape(all_days, LANES).T
    left = turned[:rows, :].astype(jnp.bfloat16)
    load_own.wait()
    load_exps.wait()

    def columns(owner, at, size):
        return pl.ds(pl.multiple_of(owner * piece + at, LANES), size)

    def exchange(index, hop, owner):
        held = covs.at[:, :, columns(owner, *parts[index])]
        return pltpu.make_async_remote_copy(
            src_ref=held, dst_ref=held,
            send_sem=fsend.at[index, hop], recv_sem=frecv.at[index, hop],
            device_id=(me, at_acct(hop)), device_id_type=MESH,
        )

    def loads_of(owner, index):
        span = columns(owner, *parts[index])
        cov = covs[:, :, span].astype(jnp.float32).reshape(rows, parts[index][1])
        return lax.dot_general(
            cov.astype(jnp.bfloat16), exps[:, span], (((1,), (1,)), ((), ())),
            preferred_element_type=jnp.float32,
        )

    loads = jnp.zeros((rows, own_accounts), jnp.float32)
    for index, (first, size) in enumerate(parts):
        for shift in shifts:
            direct(index, shift, there(tms - shift)).wait_recv()
        width = math.gcd(size, 1024)
        for at in range(first, first + size, width):
            tile = gathered[:, :, pl.ds(at, width)].astype(jnp.float32)
            cov = jnp.dot(
                left, tile.reshape(all_days, width).astype(jnp.bfloat16),
                preferred_element_type=jnp.float32,
            )
            covs[:, :, columns(acct, at, width)] = cov.reshape(accts, rows_dev, width).astype(
                jnp.bfloat16
            )
        for hop in range(1, accts):
            copy = exchange(index, hop, acct)
            copy.start()
            sends.append(copy)
        loads += loads_of(acct, index)
        for hop in range(1, accts):
            owner = at_acct(accts - hop)
            exchange(index, hop, owner).wait_recv()
            loads += loads_of(owner, index)
    store_cov = pltpu.make_async_copy(covs.at[acct], cov_hbm, local_sem.at[0])
    store_cov.start()

    links = links_ref[:, pl.ds(pl.multiple_of(acct * own_accounts, LANES), own_accounts)]
    house = lax.broadcasted_iota(jnp.int32, (HOUSES, own_accounts), 0)
    member = jnp.where(house == links, 1.0, 0.0)
    mine = place * accts + acct
    slots1[mine] = lax.dot_general(
        loads, member, (((1,), (1,)), ((), ())),
        precision=lax.Precision.HIGHEST, preferred_element_type=jnp.float32,
    )

    group = low * accts
    for step in range(1, group):
        other = layer * low + lax.rem(place + step // accts, low)
        copy = pltpu.make_async_remote_copy(
            src_ref=slots1.at[mine], dst_ref=slots1.at[mine],
            send_sem=send1.at[step], recv_sem=recv1.at[step],
            device_id=(other, at_acct(step % accts)), device_id_type=MESH,
        )
        copy.start()
        sends.append(copy)
    for step in range(1, group):
        sender = lax.rem(place + low - step // accts, low) * accts + at_acct(accts - step % accts)
        pltpu.make_async_remote_copy(
            src_ref=slots1.at[sender], dst_ref=slots1.at[sender],
            send_sem=send1.at[step], recv_sem=recv1.at[step],
            device_id=(me, at_acct(accts - 1)), device_id_type=MESH,
        ).wait_recv()
    slots2[layer] = jnp.sum(slots1[...], axis=0)
    layers = tms // low
    for step in range(1, layers):
        copy = pltpu.make_async_remote_copy(
            src_ref=slots2.at[layer], dst_ref=slots2.at[layer],
            send_sem=send2.at[step], recv_sem=recv2.at[step],
            device_id=(lax.rem(layer + step, layers) * low + place, acct), device_id_type=MESH,
        )
        copy.start()
        sends.append(copy)
    for step in range(1, layers):
        sender = lax.rem(layer + layers - step, layers)
        pltpu.make_async_remote_copy(
            src_ref=slots2.at[sender], dst_ref=slots2.at[sender],
            send_sem=send2.at[step], recv_sem=recv2.at[step],
            device_id=(me, at_acct(accts - 1)), device_id_type=MESH,
        ).wait_recv()
    totals_ref[...] = jnp.sum(slots2[...], axis=0)
    for copy in sends:
        copy.wait_send()
    store_cov.wait()


def hand_over(cov_ref, totals_ref, cov_out, totals_out):
    cov_out[...] = cov_ref[...]
    totals_out[...] = totals_ref[...]


def on_device(tms, accts, returns, start, exposures, links):
    days, factors = returns.shape
    own_accounts, cols = exposures.shape
    rows_dev = 8
    rows = rows_dev * accts
    low = least_divisor(tms)
    tiles = returns.reshape(days, factors // LANES, LANES).transpose(1, 0, 2)
    dma = pltpu.SemaphoreType.DMA
    cov, totals = pl.pallas_call(
        functools.partial(kernel, (tms, accts, low, rows_dev)),
        out_shape=(
            jax.ShapeDtypeStruct((rows_dev, cols), jnp.bfloat16),
            jax.ShapeDtypeStruct((rows, HOUSES), jnp.float32),
        ),
        in_specs=[
            pl.BlockSpec(memory_space=pltpu.SMEM),
            pl.BlockSpec(memory_space=pltpu.VMEM),
            pl.BlockSpec(memory_space=pl.ANY),
            pl.BlockSpec(memory_space=pl.ANY),
            pl.BlockSpec(memory_space=pl.ANY),
        ],
        out_specs=(
            pl.BlockSpec(memory_space=pl.ANY),
            pl.BlockSpec(memory_space=pltpu.VMEM),
        ),
        scratch_shapes=[
            pltpu.VMEM((factors // LANES, days, LANES), returns.dtype),
            pltpu.VMEM((own_accounts, cols), exposures.dtype),
            pltpu.VMEM((tms, days, cols // accts), returns.dtype),
            pltpu.VMEM((tms, days, LANES), jnp.bfloat16),
            pltpu.VMEM((LANES, days * tms), jnp.float32),
            pltpu.VMEM((accts, rows_dev, cols), jnp.bfloat16),
            pltpu.VMEM((low * accts, rows, HOUSES), jnp.float32),
            pltpu.VMEM((tms // low, rows, HOUSES), jnp.float32),
            dma((3,)),
            dma((2, tms)), dma((2, tms)), dma((tms,)), dma((tms,)),
            dma((2, accts)), dma((2, accts)),
            dma((low * accts,)), dma((low * accts,)),
            dma((tms // low,)), dma((tms // low,)),
        ],
        compiler_params=pltpu.CompilerParams(collective_id=0, has_side_effects=True),
        name="exposures_by_house",
    )(start, links[None, :], tiles, returns, exposures)
    return pl.pallas_call(
        hand_over,
        out_shape=(
            jax.ShapeDtypeStruct(cov.shape, cov.dtype),
            jax.ShapeDtypeStruct(totals.shape, totals.dtype),
        ),
        in_specs=[pl.BlockSpec(memory_space=pltpu.VMEM)] * 2,
        out_specs=(pl.BlockSpec(memory_space=pltpu.VMEM),) * 2,
        name="hand_over",
    )(cov, totals)


def solution(mesh):
    return jax.shard_map(
        functools.partial(on_device, mesh.shape["tm"], mesh.shape["acct"]),
        mesh=mesh,
        in_specs=(P("tm", None), P(), P("acct", "tm"), P()),
        out_specs=(P("acct", "tm"), P()),
        check_vma=False,
    )
```

profile of v0, /device:TPU:0, one launch (start us, length us, event | category | flops | bytes accessed | tf_op | source)
XLA Modules:
  0.0 46.5 jit_solution(9462521384396807808)
XLA Ops:
  1.3 43.6 %exposures_by_house.1 = (bf16[8,8192]{1,0:T(8,128)(2,1)}, f32[16,128]{1,0:T(8,128)}) custom-call(s32[1]{0:T(128)S(6)} %copy.6.start_ref, s32[1,512]{1,0:T(1,128)} %bitcast.5, bf16[1024,8,128]{2,1,0:T(8,128)(2,1)} %bitcast.4, bf16[8,131072]{1,0:T(8,128)(2,1)} %returns_hbm.1, bf16[256,8192]{1,0:T(8,128)(2,1)} %exposures_hbm.1), custom_call_target="tpu_custom_call" | custom-call | tf_op jit(solution)/shard_map/exposures_by_house/pallas_call | solution.py:234
  44.9 1.6 %hand_over.1 = (bf16[8,8192]{1,0:T(8,128)(2,1)}, f32[16,128]{1,0:T(8,128)}) custom-call(bf16[8,8192]{1,0:T(8,128)(2,1)} %get-tuple-element.4.cov_ref, f32[16,128]{1,0:T(8,128)} %get-tuple-element.5.totals_ref), custom_call_target="tpu_custom_call" | custom-call | tf_op jit(solution)/shard_map/hand_over/pallas_call | solution.py:269
where the time goes:
time: 46.7 us; the launch traced here: 46.5 us
  Pallas kernels  45.2 us (97%)
  between operations  1.28 us (3%)
    pallas_call x1, Pallas kernels, on_device(): pl.pallas_call(functools.partial(kernel, (tms, accts, low, rows_dev)), ou...  43.6 us
    pallas_call x1, Pallas kernels, on_device(): pl.pallas_call(hand_over, out_shape=(jax.ShapeDtypeStruct(cov.shape, cov....  1.57 us

commit v1 on v0

--- a/solution.py
+++ b/solution.py
@@ -17,15 +17,26 @@
     return min((d for d in range(2, count + 1) if count % d == 0), default=1)
 
 
+def flip(value, mask):
+    bit = 1
+    while bit <= mask:
+        if mask & bit:
+            value = value + bit * (1 - 2 * lax.rem(value // bit, 2))
+        bit *= 2
+    return value
+
+
 def kernel(
     sizes,
     start_ref, links_ref, tiles_hbm, returns_hbm, exposures_hbm,
     cov_hbm, totals_ref,
-    tiles, exps, gathered, blocks, turned, covs, slots1, slots2,
-    local_sem, dsend, drecv, bsend, brecv, fsend, frecv, send1, recv1, send2, recv2,
+    tiles, exps, gathered, blocks, turned, sent, received, covs, slots1, slots2,
+    local_sem, own_sem, dsend, drecv, bsend, brecv, zsend, zrecv, fsend, frecv,
+    send1, recv1, send2, recv2,
 ):
-    tms, accts, low, rows_dev = sizes
+    tms, accts, low, near, parts, rows_dev = sizes
     days, factors = returns_hbm.shape
+    depth = tms // near
     all_days = days * tms
     rows = rows_dev * accts
     cols = factors // tms
@@ -33,31 +44,71 @@
     own_accounts = exps.shape[0]
     me, acct = lax.axis_index("tm"), lax.axis_index("acct")
     place, layer = lax.rem(me, low), me // low
-
-    def there(shift):
-        return lax.rem(me + shift, tms)
+    member, level = lax.rem(me, near), me // near
 
     def at_acct(shift):
         return lax.rem(acct + shift, accts)
 
-    own_cols = pl.ds(pl.multiple_of(me * cols + acct * piece, LANES), piece)
+    def peer(mask):
+        return level * near + flip(member, mask)
+
+    def above(mask):
+        return flip(level, mask) * near + member
+
+    def span_of(owner, at, size):
+        return pl.ds(pl.multiple_of(owner * cols + acct * piece + at, LANES), size)
+
+    masks = range(1, near)
+    hops = [1 << bit for bit in range(depth.bit_length() - 1)]
     load_tiles = pltpu.make_async_copy(tiles_hbm, tiles, local_sem.at[2])
     load_tiles.start()
-    load_own = pltpu.make_async_copy(returns_hbm.at[:, own_cols], gathered.at[me], local_sem.at[0])
-    load_own.start()
-    load_exps = pltpu.make_async_copy(exposures_hbm, exps, local_sem.at[1])
-    load_exps.start()
+    loads_own = []
+    for r in reversed(range(depth)):
+        owner = flip(level, r) * near + member
+        copy = pltpu.make_async_copy(
+            returns_hbm.at[:, span_of(owner, 0, piece)], gathered.at[member, r], own_sem.at[r]
+        )
+        copy.start()
+        loads_own.append(copy)
 
     barrier = pltpu.get_barrier_semaphore()
     greeted = 0
-    for shift in range(1, tms):
-        pl.semaphore_signal(barrier, inc=1, device_id=(there(shift), acct), device_id_type=MESH)
+    for mask in masks:
+        pl.semaphore_signal(barrier, inc=1, device_id=(peer(mask), acct), device_id_type=MESH)
+        greeted += 1
+    for hop in hops:
+        pl.semaphore_signal(barrier, inc=1, device_id=(above(hop), acct), device_id_type=MESH)
         greeted += 1
     for step in range(low):
         for hop in range(1, accts):
             other = layer * low + lax.rem(place + step, low)
             pl.semaphore_signal(barrier, inc=1, device_id=(other, at_acct(hop)), device_id_type=MESH)
             greeted += 1
+    load_exps = pltpu.make_async_copy(exposures_hbm, exps, local_sem.at[1])
+    load_exps.start()
+    pl.semaphore_wait(barrier, greeted)
+
+    chunks = [(r, index) for r in reversed(range(depth)) for index in range(len(parts))]
+    order = [mask for mask in masks if mask >= low] + [mask for mask in masks if mask < low]
+    sends = []
+
+    def raw(r, index, mask, source):
+        at, size = parts[index]
+        owner = flip(level, r) * near + flip(member, mask)
+        return pltpu.make_async_remote_copy(
+            src_ref=returns_hbm.at[:, span_of(owner, at, size)],
+            dst_ref=gathered.at[source, r, :, pl.ds(at, size)],
+            send_sem=dsend.at[r, index, mask], recv_sem=drecv.at[r, index, mask],
+            device_id=(peer(mask), acct), device_id_type=MESH,
+        )
+
+    def start_raw(r, index):
+        for mask in order:
+            copy = raw(r, index, mask, member)
+            copy.start()
+            sends.append(copy)
+
+    start_raw(*chunks[0])
 
     load_tiles.wait()
     tile_count = tiles.shape[0]
@@ -78,51 +129,26 @@
         raw_weight(lax.broadcasted_iota(jnp.int32, (days, all_days), 1)), axis=1, keepdims=True
     )
     weights = raw_weight(me * days + lax.broadcasted_iota(jnp.int32, (days, LANES), 0)) / total
-    blocks[me] = (picked * weights).astype(jnp.bfloat16)
-
-    pl.semaphore_wait(barrier, greeted)
-
-    shifts = [*range(tms // 2, tms), *range(tms // 2 - 1, 0, -1)]
-    sends = []
-    for shift in shifts:
-        copy = pltpu.make_async_remote_copy(
-            src_ref=blocks.at[me], dst_ref=blocks.at[me],
-            send_sem=bsend.at[shift], recv_sem=brecv.at[shift],
-            device_id=(there(shift), acct), device_id_type=MESH,
-        )
+    blocks[member] = (picked * weights).astype(jnp.bfloat16)
+
+    def block_copy(mask, slot):
+        return pltpu.make_async_remote_copy(
+            src_ref=blocks.at[slot], dst_ref=blocks.at[slot],
+            send_sem=bsend.at[mask], recv_sem=brecv.at[mask],
+            device_id=(peer(mask), acct), device_id_type=MESH,
+        )
+
+    for mask in order:
+        copy = block_copy(mask, member)
         copy.start()
         sends.append(copy)
-    last = max(LANES, piece // 2 // LANES * LANES)
-    parts = [(at, size) for at, size in ((0, piece - last), (piece - last, last)) if size]
-
-    def direct(index, shift, slot):
-        at, size = parts[index]
-        to = there(shift)
-        return pltpu.make_async_remote_copy(
-            src_ref=returns_hbm.at[
-                :, pl.ds(pl.multiple_of(to * cols + acct * piece + at, LANES), size)
-            ],
-            dst_ref=gathered.at[slot, :, pl.ds(at, size)],
-            send_sem=dsend.at[index, shift], recv_sem=drecv.at[index, shift],
-            device_id=(to, acct), device_id_type=MESH,
-        )
-
-    for index in range(len(parts)):
-        for shift in shifts:
-            copy = direct(index, shift, me)
-            copy.start()
-            sends.append(copy)
-
-    for shift in shifts:
-        block = blocks.at[there(tms - shift)]
-        pltpu.make_async_remote_copy(
-            src_ref=block, dst_ref=block, send_sem=bsend.at[shift], recv_sem=brecv.at[shift],
-            device_id=(there(shift), acct), device_id_type=MESH,
-        ).wait_recv()
-    turned[...] = blocks[...].astype(jnp.float32).reshape(all_days, LANES).T
+    for chunk in chunks[1:]:
+        start_raw(*chunk)
+
+    for mask in masks:
+        block_copy(mask, flip(member, mask)).wait_recv()
+    turned[...] = blocks[...].astype(jnp.float32).reshape(days * near, LANES).T
     left = turned[:rows, :].astype(jnp.bfloat16)
-    load_own.wait()
-    load_exps.wait()
 
     def columns(owner, at, size):
         return pl.ds(pl.multiple_of(owner * piece + at, LANES), size)
@@ -143,25 +169,55 @@
             preferred_element_type=jnp.float32,
         )
 
-    loads = jnp.zeros((rows, own_accounts), jnp.float32)
-    for index, (first, size) in enumerate(parts):
-        for shift in shifts:
-            direct(index, shift, there(tms - shift)).wait_recv()
+    def partial(r, index):
+        at, size = parts[index]
+        held = pl.ds(at, size)
+        hop = r & -r
+        return pltpu.make_async_remote_copy(
+            src_ref=sent.at[r - 1, :, held], dst_ref=received.at[r - 1, :, held],
+            send_sem=zsend.at[r, index], recv_sem=zrecv.at[r, index],
+            device_id=(above(hop), acct), device_id_type=MESH,
+        )
+
+    for r, index in chunks:
+        first, size = parts[index]
+        if index == 0:
+            loads_own[depth - 1 - r].wait()
+        for mask in masks:
+            raw(r, index, mask, flip(member, mask)).wait_recv()
+        arrivals = [r + hop for hop in hops if r == 0 or hop < (r & -r)]
+        for arrival in reversed(arrivals):
+            partial(arrival, index).wait_recv()
         width = math.gcd(size, 1024)
         for at in range(first, first + size, width):
-            tile = gathered[:, :, pl.ds(at, width)].astype(jnp.float32)
+            tile = gathered[:, r, :, pl.ds(at, width)].astype(jnp.float32)
             cov = jnp.dot(
-                left, tile.reshape(all_days, width).astype(jnp.bfloat16),
+                left, tile.reshape(days * near, width).astype(jnp.bfloat16),
                 preferred_element_type=jnp.float32,
             )
-            covs[:, :, columns(acct, at, width)] = cov.reshape(accts, rows_dev, width).astype(
-                jnp.bfloat16
-            )
-        for hop in range(1, accts):
-            copy = exchange(index, hop, acct)
+            for arrival in arrivals:
+                cov += received[arrival - 1, :, pl.ds(at, width)].astype(jnp.float32)
+            if r:
+                sent[r - 1, :, pl.ds(at, width)] = cov.astype(jnp.bfloat16)
+            else:
+                covs[:, :, columns(acct, at, width)] = cov.reshape(accts, rows_dev, width).astype(
+                    jnp.bfloat16
+                )
+        if r:
+            copy = partial(r, index)
             copy.start()
             sends.append(copy)
+        else:
+            for hop in range(1, accts):
+                copy = exchange(index, hop, acct)
+                copy.start()
+                sends.append(copy)
+
+    load_exps.wait()
+    loads = jnp.zeros((rows, own_accounts), jnp.float32)
+    for index in range(len(parts)):
         loads += loads_of(acct, index)
+    for index in range(len(parts)):
         for hop in range(1, accts):
             owner = at_acct(accts - hop)
             exchange(index, hop, owner).wait_recv()
@@ -171,10 +227,10 @@
 
     links = links_ref[:, pl.ds(pl.multiple_of(acct * own_accounts, LANES), own_accounts)]
     house = lax.broadcasted_iota(jnp.int32, (HOUSES, own_accounts), 0)
-    member = jnp.where(house == links, 1.0, 0.0)
+    in_house = jnp.where(house == links, 1.0, 0.0)
     mine = place * accts + acct
     slots1[mine] = lax.dot_general(
-        loads, member, (((1,), (1,)), ((), ())),
+        loads, in_house, (((1,), (1,)), ((), ())),
         precision=lax.Precision.HIGHEST, preferred_element_type=jnp.float32,
     )
 
@@ -229,10 +285,16 @@
     rows_dev = 8
     rows = rows_dev * accts
     low = least_divisor(tms)
+    near = low * least_divisor(tms // low)
+    depth = tms // near
+    piece = cols // accts
+    last = max(LANES, piece // 2 // LANES * LANES)
+    parts = [(at, size) for at, size in ((0, piece - last), (piece - last, last)) if size]
     tiles = returns.reshape(days, factors // LANES, LANES).transpose(1, 0, 2)
     dma = pltpu.SemaphoreType.DMA
+    count = len(parts)
     cov, totals = pl.pallas_call(
-        functools.partial(kernel, (tms, accts, low, rows_dev)),
+        functools.partial(kernel, (tms, accts, low, near, parts, rows_dev)),
         out_shape=(
             jax.ShapeDtypeStruct((rows_dev, cols), jnp.bfloat16),
             jax.ShapeDtypeStruct((rows, HOUSES), jnp.float32),
@@ -251,15 +313,18 @@
         scratch_shapes=[
             pltpu.VMEM((factors // LANES, days, LANES), returns.dtype),
             pltpu.VMEM((own_accounts, cols), exposures.dtype),
-            pltpu.VMEM((tms, days, cols // accts), returns.dtype),
-            pltpu.VMEM((tms, days, LANES), jnp.bfloat16),
-            pltpu.VMEM((LANES, days * tms), jnp.float32),
+            pltpu.VMEM((near, depth, days, piece), returns.dtype),
+            pltpu.VMEM((near, days, LANES), jnp.bfloat16),
+            pltpu.VMEM((LANES, days * near), jnp.float32),
+            pltpu.VMEM((max(depth - 1, 1), rows, piece), jnp.bfloat16),
+            pltpu.VMEM((max(depth - 1, 1), rows, piece), jnp.bfloat16),
             pltpu.VMEM((accts, rows_dev, cols), jnp.bfloat16),
             pltpu.VMEM((low * accts, rows, HOUSES), jnp.float32),
             pltpu.VMEM((tms // low, rows, HOUSES), jnp.float32),
-            dma((3,)),
-            dma((2, tms)), dma((2, tms)), dma((tms,)), dma((tms,)),
-            dma((2, accts)), dma((2, accts)),
+            dma((3,)), dma((depth,)),
+            dma((depth, count, near)), dma((depth, count, near)), dma((near,)), dma((near,)),
+            dma((depth, count)), dma((depth, count)),
+            dma((count, accts)), dma((count, accts)),
             dma((low * accts,)), dma((low * accts,)),
             dma((tms // low,)), dma((tms // low,)),
         ],

time: 46.7 us -> 37.2 us (0.80)
  Pallas kernels: 45.2 us -> 35.7 us
    pallas_call x1, Pallas kernels: 43.6 us -> 34.2 us  [on_device(): pl.pallas_call(functools.partial(kernel, (tms, accts, low, near, parts, r...]
where the time goes in v1:
time: 37.2 us; the launch traced here: 37 us
  Pallas kernels  35.7 us (96%)
  between operations  1.28 us (3%)
    pallas_call x1, Pallas kernels, on_device(): pl.pallas_call(functools.partial(kernel, (tms, accts, low, near, parts, r...  34.2 us
    pallas_call x1, Pallas kernels, on_device(): pl.pallas_call(hand_over, out_shape=(jax.ShapeDtypeStruct(cov.shape, cov....  1.57 us

profile of v1, /device:TPU:0, one launch (start us, length us, event | category | flops | bytes accessed | tf_op | source)
XLA Modules:
  0.0 37.0 jit_solution(2378490773113634802)
XLA Ops:
  1.3 34.2 %exposures_by_house.1 = (bf16[8,8192]{1,0:T(8,128)(2,1)}, f32[16,128]{1,0:T(8,128)}) custom-call(s32[1]{0:T(128)S(6)} %copy.6.start_ref, s32[1,512]{1,0:T(1,128)} %bitcast.5, bf16[1024,8,128]{2,1,0:T(8,128)(2,1)} %bitcast.4, bf16[8,131072]{1,0:T(8,128)(2,1)} %returns_hbm.1, bf16[256,8192]{1,0:T(8,128)(2,1)} %exposures_hbm.1), custom_call_target="tpu_custom_call" | custom-call | tf_op jit(solution)/shard_map/exposures_by_house/pallas_call | solution.py:296
  35.4 1.6 %hand_over.1 = (bf16[8,8192]{1,0:T(8,128)(2,1)}, f32[16,128]{1,0:T(8,128)}) custom-call(bf16[8,8192]{1,0:T(8,128)(2,1)} %get-tuple-element.4.cov_ref, f32[16,128]{1,0:T(8,128)} %get-tuple-element.5.totals_ref), custom_call_target="tpu_custom_call" | custom-call | tf_op jit(solution)/shard_map/hand_over/pallas_call | solution.py:334

commit v2 on v1

--- a/solution.py
+++ b/solution.py
@@ -10,6 +10,8 @@
 
 HOUSES = 128
 LANES = 128
+PARTS = 4
+VMEM_LIMIT = 40 * 2**20
 MESH = pl.DeviceIdType.MESH
 
 
@@ -28,9 +30,9 @@
 
 def kernel(
     sizes,
-    start_ref, links_ref, tiles_hbm, returns_hbm, exposures_hbm,
-    cov_hbm, totals_ref,
-    tiles, exps, gathered, blocks, turned, sent, received, covs, slots1, slots2,
+    start_ref, links_hbm, tiles_hbm, returns_hbm, exposures_hbm,
+    cov_ref, totals_ref,
+    links_ref, tiles, exps, by_house, gathered, blocks, turned, sent, received, covs, slots1, slots2,
     local_sem, own_sem, dsend, drecv, bsend, brecv, zsend, zrecv, fsend, frecv,
     send1, recv1, send2, recv2,
 ):
@@ -60,17 +62,6 @@
 
     masks = range(1, near)
     hops = [1 << bit for bit in range(depth.bit_length() - 1)]
-    load_tiles = pltpu.make_async_copy(tiles_hbm, tiles, local_sem.at[2])
-    load_tiles.start()
-    loads_own = []
-    for r in reversed(range(depth)):
-        owner = flip(level, r) * near + member
-        copy = pltpu.make_async_copy(
-            returns_hbm.at[:, span_of(owner, 0, piece)], gathered.at[member, r], own_sem.at[r]
-        )
-        copy.start()
-        loads_own.append(copy)
-
     barrier = pltpu.get_barrier_semaphore()
     greeted = 0
     for mask in masks:
@@ -84,6 +75,18 @@
             other = layer * low + lax.rem(place + step, low)
             pl.semaphore_signal(barrier, inc=1, device_id=(other, at_acct(hop)), device_id_type=MESH)
             greeted += 1
+    load_tiles = pltpu.make_async_copy(tiles_hbm, tiles, local_sem.at[2])
+    load_tiles.start()
+    loads_own = []
+    for r in reversed(range(depth)):
+        owner = flip(level, r) * near + member
+        copy = pltpu.make_async_copy(
+            returns_hbm.at[:, span_of(owner, 0, piece)], gathered.at[member, r], own_sem.at[r]
+        )
+        copy.start()
+        loads_own.append(copy)
+    load_links = pltpu.make_async_copy(links_hbm, links_ref, local_sem.at[0])
+    load_links.start()
     load_exps = pltpu.make_async_copy(exposures_hbm, exps, local_sem.at[1])
     load_exps.start()
     pl.semaphore_wait(barrier, greeted)
@@ -161,11 +164,27 @@
             device_id=(me, at_acct(hop)), device_id_type=MESH,
         )
 
+    load_links.wait()
+    load_exps.wait()
+    links = links_ref[:, pl.ds(pl.multiple_of(acct * own_accounts, LANES), own_accounts)]
+    house = lax.broadcasted_iota(jnp.int32, (HOUSES, own_accounts), 0)
+    in_house = jnp.where(house == links, 1.0, 0.0).astype(jnp.bfloat16)
+    unit = math.gcd(cols, 512)
+    units = cols // unit
+
+    def sum_houses(first, last):
+        for at in range(first * unit, last * unit, unit):
+            held = pl.ds(at, unit)
+            summed = jnp.dot(in_house, exps[:, held], preferred_element_type=jnp.float32)
+            high = summed.astype(jnp.bfloat16)
+            by_house[:HOUSES, held] = high
+            by_house[HOUSES:, held] = (summed - high.astype(jnp.float32)).astype(jnp.bfloat16)
+
     def loads_of(owner, index):
         span = columns(owner, *parts[index])
         cov = covs[:, :, span].astype(jnp.float32).reshape(rows, parts[index][1])
         return lax.dot_general(
-            cov.astype(jnp.bfloat16), exps[:, span], (((1,), (1,)), ((), ())),
+            cov.astype(jnp.bfloat16), by_house[:, span], (((1,), (1,)), ((), ())),
             preferred_element_type=jnp.float32,
         )
 
@@ -179,7 +198,9 @@
             device_id=(above(hop), acct), device_id_type=MESH,
         )
 
-    for r, index in chunks:
+    loads = jnp.zeros((rows, 2 * HOUSES), jnp.float32)
+    early = (depth - 1) * len(parts)
+    for count, (r, index) in enumerate(chunks):
         first, size = parts[index]
         if index == 0:
             loads_own[depth - 1 - r].wait()
@@ -207,32 +228,20 @@
             copy = partial(r, index)
             copy.start()
             sends.append(copy)
+            sum_houses(units * count // early, units * (count + 1) // early)
         else:
             for hop in range(1, accts):
                 copy = exchange(index, hop, acct)
                 copy.start()
                 sends.append(copy)
-
-    load_exps.wait()
-    loads = jnp.zeros((rows, own_accounts), jnp.float32)
-    for index in range(len(parts)):
-        loads += loads_of(acct, index)
+            loads += loads_of(acct, index)
     for index in range(len(parts)):
         for hop in range(1, accts):
             owner = at_acct(accts - hop)
             exchange(index, hop, owner).wait_recv()
             loads += loads_of(owner, index)
-    store_cov = pltpu.make_async_copy(covs.at[acct], cov_hbm, local_sem.at[0])
-    store_cov.start()
-
-    links = links_ref[:, pl.ds(pl.multiple_of(acct * own_accounts, LANES), own_accounts)]
-    house = lax.broadcasted_iota(jnp.int32, (HOUSES, own_accounts), 0)
-    in_house = jnp.where(house == links, 1.0, 0.0)
     mine = place * accts + acct
-    slots1[mine] = lax.dot_general(
-        loads, in_house, (((1,), (1,)), ((), ())),
-        precision=lax.Precision.HIGHEST, preferred_element_type=jnp.float32,
-    )
+    slots1[mine] = loads[:, :HOUSES] + loads[:, HOUSES:]
 
     group = low * accts
     for step in range(1, group):
@@ -244,6 +253,7 @@
         )
         copy.start()
         sends.append(copy)
+    cov_ref[...] = covs[acct]
     for step in range(1, group):
         sender = lax.rem(place + low - step // accts, low) * accts + at_acct(accts - step % accts)
         pltpu.make_async_remote_copy(
@@ -271,7 +281,6 @@
     totals_ref[...] = jnp.sum(slots2[...], axis=0)
     for copy in sends:
         copy.wait_send()
-    store_cov.wait()
 
 
 def hand_over(cov_ref, totals_ref, cov_out, totals_out):
@@ -288,9 +297,10 @@
     near = low * least_divisor(tms // low)
     depth = tms // near
     piece = cols // accts
-    last = max(LANES, piece // 2 // LANES * LANES)
-    parts = [(at, size) for at, size in ((0, piece - last), (piece - last, last)) if size]
+    width = max(LANES, piece // PARTS // LANES * LANES)
+    parts = [(at, min(width, piece - at)) for at in range(0, piece, width)]
     tiles = returns.reshape(days, factors // LANES, LANES).transpose(1, 0, 2)
+    held = functools.partial(pltpu.with_memory_space_constraint, memory_space=pltpu.HBM)
     dma = pltpu.SemaphoreType.DMA
     count = len(parts)
     cov, totals = pl.pallas_call(
@@ -301,18 +311,17 @@
         ),
         in_specs=[
             pl.BlockSpec(memory_space=pltpu.SMEM),
-            pl.BlockSpec(memory_space=pltpu.VMEM),
+            pl.BlockSpec(memory_space=pl.ANY),
             pl.BlockSpec(memory_space=pl.ANY),
             pl.BlockSpec(memory_space=pl.ANY),
             pl.BlockSpec(memory_space=pl.ANY),
         ],
-        out_specs=(
-            pl.BlockSpec(memory_space=pl.ANY),
-            pl.BlockSpec(memory_space=pltpu.VMEM),
-        ),
+        out_specs=(pl.BlockSpec(memory_space=pltpu.VMEM),) * 2,
         scratch_shapes=[
+            pltpu.VMEM((1, links.size), jnp.int32),
             pltpu.VMEM((factors // LANES, days, LANES), returns.dtype),
             pltpu.VMEM((own_accounts, cols), exposures.dtype),
+            pltpu.VMEM((2 * HOUSES, cols), jnp.bfloat16),
             pltpu.VMEM((near, depth, days, piece), returns.dtype),
             pltpu.VMEM((near, days, LANES), jnp.bfloat16),
             pltpu.VMEM((LANES, days * near), jnp.float32),
@@ -328,9 +337,11 @@
             dma((low * accts,)), dma((low * accts,)),
             dma((tms // low,)), dma((tms // low,)),
         ],
-        compiler_params=pltpu.CompilerParams(collective_id=0, has_side_effects=True),
+        compiler_params=pltpu.CompilerParams(
+            collective_id=0, has_side_effects=True, vmem_limit_bytes=VMEM_LIMIT
+        ),
         name="exposures_by_house",
-    )(start, links[None, :], tiles, returns, exposures)
+    )(start, *(held(array) for array in (links[None, :], tiles, returns, exposures)))
     return pl.pallas_call(
         hand_over,
         out_shape=(
@@ -339,6 +350,7 @@
         ),
         in_specs=[pl.BlockSpec(memory_space=pltpu.VMEM)] * 2,
         out_specs=(pl.BlockSpec(memory_space=pltpu.VMEM),) * 2,
+        compiler_params=pltpu.CompilerParams(vmem_limit_bytes=VMEM_LIMIT),
         name="hand_over",
     )(cov, totals)
 

time: 37.2 us -> 35.4 us (0.952)
  Pallas kernels: 35.7 us -> 34 us
    pallas_call x1, Pallas kernels: 1.57 us -> 0.67 us  [on_device(): pl.pallas_call(hand_over, out_shape=(jax.ShapeDtypeStruct(cov.shape, cov....]
    pallas_call x1, Pallas kernels: 34.2 us -> 33.3 us  [on_device(): pl.pallas_call(functools.partial(kernel, (tms, accts, low, near, parts, r...]
where the time goes in v2:
time: 35.4 us; the launch traced here: 35.3 us
  Pallas kernels  34 us (96%)
  between operations  1.28 us (4%)
    pallas_call x1, Pallas kernels, on_device(): pl.pallas_call(functools.partial(kernel, (tms, accts, low, near, parts, r...  33.3 us

profile of v2, /device:TPU:0, one launch (start us, length us, event | category | flops | bytes accessed | tf_op | source)
XLA Modules:
  0.0 35.3 jit_solution(5431662225354502658)
XLA Ops:
  1.3 33.3 %exposures_by_house.1 = (bf16[8,8192]{1,0:T(8,128)(2,1)S(1)}, f32[16,128]{1,0:T(8,128)S(1)}) custom-call(s32[1]{0:T(128)S(6)} %copy.6.start_ref, s32[1,512]{1,0:T(1,128)} %bitcast.5, bf16[1024,8,128]{2,1,0:T(8,128)(2,1)} %bitcast.4, bf16[8,131072]{1,0:T(8,128)(2,1)} %returns_hbm.1, bf16[256,8192]{1,0:T(8,128)(2,1)} %exposures_hbm.1), custom_call_target="tpu_custom_call" | custom-call | tf_op jit(solution)/shard_map/exposures_by_house/pallas_call | solution.py:306
  34.6 0.7 %hand_over.1 = (bf16[8,8192]{1,0:T(8,128)(2,1)}, f32[16,128]{1,0:T(8,128)}) custom-call(bf16[8,8192]{1,0:T(8,128)(2,1)S(1)} %get-tuple-element.4.cov_ref, f32[16,128]{1,0:T(8,128)S(1)} %get-tuple-element.5.totals_ref), custom_call_target="tpu_custom_call" | custom-call | tf_op jit(solution)/shard_map/hand_over/pallas_call | solution.py:345

commit v3 on v2

--- a/solution.py
+++ b/solution.py
@@ -10,7 +10,7 @@
 
 HOUSES = 128
 LANES = 128
-PARTS = 4
+PARTS = 2
 VMEM_LIMIT = 40 * 2**20
 MESH = pl.DeviceIdType.MESH
 

time: 35.4 us -> 35 us (0.989)
  Pallas kernels: 34 us -> 33.5 us
    pallas_call x1, Pallas kernels: 33.3 us -> 32.8 us  [on_device(): pl.pallas_call(functools.partial(kernel, (tms, accts, low, near, parts, r...]
where the time goes in v3:
time: 35 us; the launch traced here: 34.8 us
  Pallas kernels  33.5 us (96%)
  between operations  1.28 us (4%)
    pallas_call x1, Pallas kernels, on_device(): pl.pallas_call(functools.partial(kernel, (tms, accts, low, near, parts, r...  32.8 us

profile of v3, /device:TPU:0, one launch (start us, length us, event | category | flops | bytes accessed | tf_op | source)
XLA Modules:
  0.0 34.8 jit_solution(15048836306117110180)
XLA Ops:
  1.3 32.8 %exposures_by_house.1 = (bf16[8,8192]{1,0:T(8,128)(2,1)S(1)}, f32[16,128]{1,0:T(8,128)S(1)}) custom-call(s32[1]{0:T(128)S(6)} %copy.6.start_ref, s32[1,512]{1,0:T(1,128)} %bitcast.5, bf16[1024,8,128]{2,1,0:T(8,128)(2,1)} %bitcast.4, bf16[8,131072]{1,0:T(8,128)(2,1)} %returns_hbm.1, bf16[256,8192]{1,0:T(8,128)(2,1)} %exposures_hbm.1), custom_call_target="tpu_custom_call" | custom-call | tf_op jit(solution)/shard_map/exposures_by_house/pallas_call | solution.py:306
  34.1 0.7 %hand_over.1 = (bf16[8,8192]{1,0:T(8,128)(2,1)}, f32[16,128]{1,0:T(8,128)}) custom-call(bf16[8,8192]{1,0:T(8,128)(2,1)S(1)} %get-tuple-element.4.cov_ref, f32[16,128]{1,0:T(8,128)S(1)} %get-tuple-element.5.totals_ref), custom_call_target="tpu_custom_call" | custom-call | tf_op jit(solution)/shard_map/hand_over/pallas_call | solution.py:345
